TPU v7x, 32 devices: a whole 2x2x4 slice. The times are simulated.
32 devices in a mesh: section: 2 (over y), expert: 4 (over z), dp: 4 (over x, core).
Axes of the slice: x: 2, y: 2, z: 4, core: 2. Of those that a mesh axis runs over, the one named last changes fastest.
Arguments:
- residual: bfloat16 [4096, 2048], P(('section', 'expert', 'dp')), may hold values from -12 to 12
- queries: bfloat16 [4096, 1024], P(('section', 'expert', 'dp')), may hold values from -6 to 6
- attn_keys: bfloat16 [4096, 1024], P(('section', 'expert', 'dp')), may hold values from -6 to 6
- attn_values: bfloat16 [4096, 1024], P(('section', 'expert', 'dp')), may hold values from -6 to 6
- out_weight: bfloat16 [1024, 2048], P('expert'), may hold values from -0.1875 to 0.1875
- norm_gain: float32 [2048], replicated, may hold values from 0.25 to 1.75
- gate_weight: bfloat16 [4, 2048, 4096], P('expert', None, 'dp'), may hold values from -0.125 to 0.125
- up_weight: bfloat16 [4, 2048, 4096], P('expert', None, 'dp'), may hold values from -0.125 to 0.125
- down_weight: bfloat16 [4, 4096, 2048], P('expert', 'dp'), may hold values from -0.09375 to 0.09375
- expert_ids: int32 [4096, 1], P(('section', 'expert', 'dp')), may hold values from 0 to 3; in each aligned block of 128 rows (0 to 127, 128 to 255, ...) at most 64 rows name the same one
- out_grad: bfloat16 [4096, 2048], P(('section', 'expert', 'dp')), may hold values from -6 to 6
Outputs:
- layer_out: bfloat16 [4096, 2048], P(('section', 'expert', 'dp'))
- resid_grad: bfloat16 [4096, 2048], P(('section', 'expert', 'dp'))
- query_grad: bfloat16 [4096, 1024], P(('section', 'expert', 'dp'))
- key_grad: bfloat16 [4096, 1024], P(('section', 'expert', 'dp'))
- value_grad: bfloat16 [4096, 1024], P(('section', 'expert', 'dp'))
- weight_grad: float32 [1024, 2048], P('expert')
Inputs may be any that keep to these rules, and one draw needn't show every extreme that they name: `expert_ids`: no expert is named by more than 64 of the 128 rows of one device (an aligned block); in every draw some block names one expert exactly 64 times.
All inputs are finite; a program needn't handle non-finite values.
Results may differ from a plain program's by a relative error of at most 0.023.
Values may be sent and summed in bfloat16 or wider, within the bound.
A program may use at most 128 MiB of HBM per device.

v0:
```python
import math
import jax
import jax.numpy as jnp
from jax import lax
from jax.sharding import PartitionSpec as P

D = 2048
HEADS = 8
HEAD = 128
A = 1024
FF = 4096
epsilon = 1e-06


def contract_last(left_side, right_side):
    return lax.dot_general(
        left_side, right_side, (((1,), (1,)), ((), ())), preferred_element_type=jnp.float32
    )


def contract_first(left_side, right_side):
    return lax.dot_general(
        left_side, right_side, (((0,), (0,)), ((), ())), preferred_element_type=jnp.float32
    )


def shards(
    residual,
    queries,
    attn_keys,
    attn_values,
    out_weight,
    norm_gain,
    gate_weight,
    up_weight,
    down_weight,
    expert_ids,
    out_grad,
):
    tokens_here = residual.shape[0]
    experts = lax.axis_size("expert")
    data_ways = lax.axis_size("dp")
    capacity = max(tokens_here // 8, 2 * tokens_here // experts)
    inv_root = 1.0 / math.sqrt(HEAD)
    keys_all, values_all = (
        lax.all_gather(attn_keys, "dp", axis=0, tiled=True),
        lax.all_gather(attn_values, "dp", axis=0, tiled=True),
    )
    query_heads = queries.reshape(tokens_here, HEADS, HEAD)
    key_heads = keys_all.reshape(-1, HEADS, HEAD)
    value_heads = values_all.reshape(-1, HEADS, HEAD)
    scores = (
        jnp.einsum("thd,shd->hts", query_heads, key_heads, preferred_element_type=jnp.float32)
        * inv_root
    )
    row_peak = jnp.max(scores, axis=-1, keepdims=True)
    exp_scores = jnp.exp(scores - row_peak)
    attn_probs = exp_scores / jnp.sum(exp_scores, axis=-1, keepdims=True)
    probs_low = attn_probs.astype(jnp.bfloat16)
    attended = (
        jnp.einsum("hts,shd->thd", probs_low, value_heads, preferred_element_type=jnp.float32)
        .reshape(tokens_here, A)
        .astype(jnp.bfloat16)
    )
    full_out = lax.all_gather(out_weight, "expert", axis=0, tiled=True)
    hidden = residual.astype(jnp.float32) + jnp.dot(
        attended, full_out, preferred_element_type=jnp.float32
    )
    inv_rms = lax.rsqrt(jnp.mean(hidden * hidden, axis=-1, keepdims=True) + epsilon)
    unit_rows = hidden * inv_rms
    normed = (unit_rows * norm_gain).astype(jnp.bfloat16)
    expert_of = expert_ids[:, 0]
    onehot = (expert_of[:, None] == jnp.arange(experts, dtype=jnp.int32)[None, :]).astype(
        jnp.bfloat16
    )
    row_iota = jnp.arange(tokens_here, dtype=jnp.int32)
    earlier_mask = (row_iota[:, None] > row_iota[None, :]).astype(jnp.bfloat16)
    earlier = jnp.dot(earlier_mask, onehot, preferred_element_type=jnp.float32)
    rank_index = jnp.sum(earlier * onehot.astype(jnp.float32), axis=1).astype(jnp.int32)
    slot_index = expert_of * capacity + rank_index
    empty_rows = jnp.zeros((experts * capacity, D), jnp.bfloat16)
    send_buffer = empty_rows.at[slot_index].set(normed).reshape(experts, capacity, D)
    gate_local = gate_weight[0]
    up_local = up_weight[0]
    down_local = down_weight[0]
    block_width = FF // data_ways
    arrived = lax.all_to_all(send_buffer, "expert", split_axis=0, concat_axis=0, tiled=True)
    piece_rows = arrived.shape[1]
    gathered = lax.all_gather(arrived, "dp", axis=0, tiled=True)
    flattened = gathered.reshape(-1, D)
    gate_pre = jnp.dot(flattened, gate_local, preferred_element_type=jnp.float32)
    up_pre = jnp.dot(flattened, up_local, preferred_element_type=jnp.float32)
    activated = (jax.nn.silu(gate_pre) * up_pre).astype(jnp.bfloat16)
    partial_out = jnp.dot(activated, down_local, preferred_element_type=jnp.float32)
    summed = lax.psum_scatter(
        partial_out.reshape(data_ways * experts, piece_rows, D).astype(jnp.bfloat16),
        "dp",
        scatter_dimension=0,
        tiled=True,
    )
    returned = lax.all_to_all(summed, "expert", split_axis=0, concat_axis=0, tiled=True)
    gate_saved = gate_pre.reshape(data_ways * experts, piece_rows, block_width)
    up_saved = up_pre.reshape(data_ways * experts, piece_rows, block_width)
    expert_back = returned.reshape(experts * capacity, D)[slot_index]
    layer_out = (hidden + expert_back.astype(jnp.float32)).astype(jnp.bfloat16)
    grad_buffer = empty_rows.at[slot_index].set(out_grad).reshape(experts, capacity, D)
    grad_arrived = lax.all_to_all(grad_buffer, "expert", split_axis=0, concat_axis=0, tiled=True)
    grad_gathered = lax.all_gather(grad_arrived, "dp", axis=0, tiled=True)
    grad_flat = grad_gathered.reshape(-1, D)
    gate_pre = gate_saved.reshape(-1, block_width)
    up_pre = up_saved.reshape(-1, block_width)
    sigmoid_gate = jax.nn.sigmoid(gate_pre)
    grad_act = contract_last(grad_flat, down_local)
    grad_gate = (grad_act * up_pre * sigmoid_gate * (1.0 + gate_pre * (1.0 - sigmoid_gate))).astype(
        jnp.bfloat16
    )
    grad_up = (grad_act * jax.nn.silu(gate_pre)).astype(jnp.bfloat16)
    partial_grad = contract_last(grad_gate, gate_local) + contract_last(grad_up, up_local)
    grad_normed_rows = lax.psum_scatter(
        partial_grad.reshape(data_ways * experts, capacity, D).astype(jnp.bfloat16),
        "dp",
        scatter_dimension=0,
        tiled=True,
    )
    grad_returned = lax.all_to_all(
        grad_normed_rows, "expert", split_axis=0, concat_axis=0, tiled=True
    )
    grad_normed = grad_returned.reshape(experts * capacity, D)[slot_index].astype(jnp.float32)
    scaled = grad_normed * norm_gain
    resid_grad = (
        out_grad.astype(jnp.float32)
        + inv_rms * (scaled - unit_rows * jnp.mean(scaled * unit_rows, axis=-1, keepdims=True))
    ).astype(jnp.bfloat16)
    grad_shard = lax.psum_scatter(
        contract_first(attended, resid_grad).astype(jnp.bfloat16),
        "expert",
        scatter_dimension=0,
        tiled=True,
    )
    weight_grad = lax.psum(grad_shard, ("section", "dp")).astype(jnp.float32)
    grad_attended = contract_last(resid_grad, full_out).astype(jnp.bfloat16)
    grad_heads = grad_attended.reshape(tokens_here, HEADS, HEAD)
    grad_probs = jnp.einsum(
        "thd,shd->hts", grad_heads, value_heads, preferred_element_type=jnp.float32
    )
    row_delta = jnp.sum(attn_probs * grad_probs, axis=-1, keepdims=True)
    grad_scores = (attn_probs * (grad_probs - row_delta)).astype(jnp.bfloat16)
    query_grad = (
        (
            jnp.einsum("hts,shd->thd", grad_scores, key_heads, preferred_element_type=jnp.float32)
            * inv_root
        )
        .reshape(tokens_here, A)
        .astype(jnp.bfloat16)
    )
    key_part = (
        jnp.einsum("hts,thd->shd", grad_scores, query_heads, preferred_element_type=jnp.float32)
        * inv_root
    )
    value_part = jnp.einsum(
        "hts,thd->shd", probs_low, grad_heads, preferred_element_type=jnp.float32
    )
    key_value = lax.psum_scatter(
        jnp.concatenate(
            [
                key_part.reshape(lax.axis_size("dp") * tokens_here, A),
                value_part.reshape(lax.axis_size("dp") * tokens_here, A),
            ],
            axis=1,
        ).astype(jnp.bfloat16),
        "dp",
        scatter_dimension=0,
        tiled=True,
    ).astype(jnp.float32)
    key_grad = key_value[:, :A].astype(jnp.bfloat16)
    value_grad = key_value[:, A:].astype(jnp.bfloat16)
    return (layer_out, resid_grad, query_grad, key_grad, value_grad, weight_grad)


def solution(mesh):
    return jax.shard_map(
        shards,
        mesh=mesh,
        in_specs=(
            P(("section", "expert", "dp"), None),
            P(("section", "expert", "dp"), None),
            P(("section", "expert", "dp"), None),
            P(("section", "expert", "dp"), None),
            P("expert", None),
            P(),
            P("expert", None, "dp"),
            P("expert", None, "dp"),
            P("expert", "dp", None),
            P(("section", "expert", "dp"), None),
            P(("section", "expert", "dp"), None),
        ),
        out_specs=(
            P(("section", "expert", "dp"), None),
            P(("section", "expert", "dp"), None),
            P(("section", "expert", "dp"), None),
            P(("section", "expert", "dp"), None),
            P(("section", "expert", "dp"), None),
            P("expert", None),
        ),
        check_vma=False,
    )
```

profile of v0, /device:TPU:0, one launch (start us, length us, event | category | flops | bytes accessed | tf_op | source)
XLA Modules:
  0.0 544.3 jit_solution(3329325886076428349)
XLA Ops:
  7.2 0.7 all-gather.8.cloned.1.call-update
  7.9 1.8 copy.38
  9.8 0.7 all-gather.10.cloned.1.call-update
  10.5 1.1 copy.51
  11.7 0.9 fusion.22
  12.6 0.7 fusion.37
  13.2 15.7 %all-gather.8.cloned.1.call-done = bf16[512,1024]{1,0:T(8,128)(2,1)} async-done(((bf16[128,1024]{1,0:T(8,128)(2,1)}), bf16[512,1024]{1,0:T(8,128)(2,1)}) %all-gather.8.cloned.1.call-update) | async-done | bytes 1048592 | tf_op jit(solution)/shard_map/all_gather | solution.py:47
  29.0 1.5 copy.41
  30.5 17.5 %all-gather.6.cloned.1.call-done = bf16[512,1024]{0,1:T(8,128)(2,1)} async-done(((bf16[128,1024]{0,1:T(8,128)(2,1)}), bf16[512,1024]{0,1:T(8,128)(2,1)}) %all-gather.6.cloned.1.call-update) | async-done | bytes 1048592 | tf_op jit(solution)/shard_map/all_gather | solution.py:46
  48.0 2.1 fusion.42
  50.1 1.4 convolution_convert_fusion.2
  51.5 78.8 %all-gather.10.cloned.1.call-done = bf16[1024,2048]{1,0:T(8,128)(2,1)} async-done(((bf16[256,2048]{1,0:T(8,128)(2,1)}), bf16[1024,2048]{1,0:T(8,128)(2,1)}) %all-gather.10.cloned.1.call-update) | async-done | bytes 4194320 | tf_op jit(solution)/shard_map/all_gather | solution.py:65
  130.3 3.2 multiply_reduce_fusion.3
  133.5 1.8 scatter_custom_fusion
  135.3 29.0 %all_to_all.20 = bf16[4,64,2048]{2,1,0:T(8,128)(2,1)} all-to-all(bf16[4,64,2048]{2,1,0:T(8,128)(2,1)S(1)} %bitcast.80), channel_id=1, replica_groups=mesh['section'=2,'expert'=4,'dp'=4] {'expert'}, dimensions={0} | all-to-all | bytes 2097152 | tf_op jit(solution)/shard_map/all_to_all | solution.py:87
  164.4 2.2 scatter_custom_fusion.1
  166.6 28.4 %all_to_all.21 = bf16[4,64,2048]{2,1,0:T(8,128)(2,1)} all-to-all(bf16[4,64,2048]{2,1,0:T(8,128)(2,1)S(1)} %bitcast.78), channel_id=1, replica_groups=mesh['section'=2,'expert'=4,'dp'=4] {'expert'}, dimensions={0} | all-to-all | bytes 2097152 | tf_op jit(solution)/shard_map/all_to_all | solution.py:107
  195.1 2.9 all-gather.12.cloned.1.call-done
  198.0 7.6 %fusion.11 = f32[1024,1024]{1,0:T(8,128)S(1)} fusion(bf16[1024,2048]{1,0:T(8,128)(2,1)} %bitcast.94, bf16[1,2048,1024]{2,1,0:T(8,128)(2,1)} %param.17), kind=kOutput, calls=%fused_computation.16 | convolution fusion | flops 4294967296 | bytes 12582912 | tf_op jit(solution)/shard_map/dot_general | solution.py:91
  205.7 6.5 %multiply_convert_fusion.2 = (bf16[1024,1024]{1,0:T(8,128)(2,1)S(1)}, f32[1024,1024]{1,0:T(8,128)}) fusion(f32[1024,1024]{1,0:T(8,128)S(1)} %fusion.11, bf16[1024,2048]{1,0:T(8,128)(2,1)S(1)} %bitcast.95, bf16[1,2048,1024]{2,1,0:T(8,128)(2,1)S(1)} %copy-done.10), kind=kOutput, calls=%fused_computation.20 | convolution fusion | flops 4301258752 | bytes 18874368 | tf_op jit(solution)/shard_map/dot_general | solution.py:92
  212.2 6.1 %fusion.14 = bf16[16,64,2048]{2,1,0:T(8,128)(2,1)} fusion(bf16[16,64,1024]{2,1,0:T(8,128)(2,1)S(1)} %bitcast.97, bf16[1,1024,2048]{2,1,0:T(8,128)(2,1)S(1)} %copy-done.9), kind=kOutput, calls=%fused_computation.24 | convolution fusion | flops 4297064448 | bytes 10485760 | tf_op jit(solution)/shard_map/dot_general | solution.py:94
  218.6 15.3 %all-gather.14.cloned.1.call-done = bf16[16,64,2048]{2,1,0:T(8,128)(2,1)} async-done(((bf16[4,64,2048]{2,1,0:T(8,128)(2,1)}), bf16[16,64,2048]{2,1,0:T(8,128)(2,1)}) %all-gather.14.cloned.1.call-update) | async-done | bytes 4194320 | tf_op jit(solution)/shard_map/all_gather | solution.py:108
  233.9 7.7 %fusion.3 = f32[1024,1024]{1,0:T(8,128)S(1)} fusion(bf16[1024,2048]{1,0:T(8,128)(2,1)} %bitcast.93, bf16[1,1024,2048]{2,1,0:T(8,128)(2,1)} %param.19), kind=kOutput, calls=%fused_computation.8 | convolution fusion | flops 4294967296 | bytes 12582912 | tf_op jit(solution)/shard_map/dot_general | solution.py:16
  241.7 6.9 %fusion.5 = f32[1024,2048]{1,0:T(8,128)} fusion(bf16[1,2048,1024]{2,1,0:T(8,128)(2,1)S(1)} %copy-done.11, f32[1024,1024]{1,0:T(8,128)S(1)} %fusion.3, f32[1024,1024]{1,0:T(8,128)S(1)} %copy-done.15), kind=kOutput, calls=%fused_computation.10 | convolution fusion | flops 4301258752 | bytes 20971520 | tf_op jit(solution)/shard_map/dot_general | solution.py:16
  248.5 14.3 %add_convert_fusion = bf16[1024,2048]{1,0:T(8,128)(2,1)} fusion(f32[1024,2048]{1,0:T(8,128)} %fusion.5, bf16[1,2048,1024]{2,1,0:T(8,128)(2,1)S(1)} %copy-done.12, f32[1024,1024]{1,0:T(8,128)} %copy-done.14, f32[1024,1024]{1,0:T(8,128)} %copy-done.16, f32[1024,1024]{1,0:T(8,128)} %get-tuple-element.33), kind=kOutput, calls=%fused_computation.5 | convolution fusion | flops 4309647360 | bytes 29360128 | tf_op jit(solution)/shard_map/dot_general | solution.py:16
  262.9 18.0 %reduce-scatter.5.cloned.1.call-done = bf16[4,64,2048]{2,1,0:T(8,128)(2,1)} async-done(((bf16[16,64,2048]{2,1,0:T(8,128)(2,1)}), bf16[4,64,2048]{2,1,0:T(8,128)(2,1)}) %reduce-scatter.5.cloned.1.call-update) | async-done | bytes 1048592 | tf_op jit(solution)/shard_map/reduce_scatter | solution.py:95
  280.9 4.6 all-to-all-start.1
  285.5 42.6 %reduce-scatter.7.cloned.1.call-done = bf16[4,64,2048]{2,1,0:T(8,128)(2,1)} async-done(((bf16[16,64,2048]{2,1,0:T(8,128)(2,1)}), bf16[4,64,2048]{2,1,0:T(8,128)(2,1)}) %reduce-scatter.7.cloned.1.call-update) | async-done | bytes 1048592 | tf_op jit(solution)/shard_map/reduce_scatter | solution.py:119
  328.1 4.6 all-to-all-start.3
  332.7 1.7 gather_fusion
  334.4 23.8 %all-to-all-done.3 = bf16[4,64,2048]{2,1,0:T(8,128)(2,1)S(1)} async-done(((bf16[4,64,2048]{2,1,0:T(8,128)(2,1)}), bf16[4,64,2048]{2,1,0:T(8,128)(2,1)S(1)}, u32[]{:S(2)}, u32[]{:S(2)}) %all-to-all-start.3) | async-done | bytes 1048608 | tf_op jit(solution)/shard_map/all_to_all | solution.py:125
  358.2 0.9 gather_fusion.1
  359.5 2.4 add_convert_fusion.1
  361.9 3.2 convolution_convert_fusion
  365.3 3.9 convolution_convert_fusion.3
  369.2 0.8 copy.52
  370.1 2.5 convolution_convert_fusion.1
  372.6 2.3 copy.47
  374.9 1.5 multiply_reduce_fusion
  377.2 1.3 copy.46
  378.5 2.8 pad_maximum_fusion
  381.5 58.7 %reduce-scatter.11.cloned.1.call-done = bf16[256,2048]{1,0:T(8,128)(2,1)} async-done(((bf16[1024,2048]{1,0:T(8,128)(2,1)}), bf16[256,2048]{1,0:T(8,128)(2,1)}) %reduce-scatter.11.cloned.1.call-update) | async-done | bytes 1048592 | tf_op jit(solution)/shard_map/reduce_scatter | solution.py:134
  440.2 0.4 fusion.21
  440.6 0.9 copy.48
  441.5 33.5 %reduce-scatter.9.cloned.1.call-done = bf16[128,2048]{1,0:T(8,128)(2,1)} async-done(((bf16[512,2048]{1,0:T(8,128)(2,1)}), bf16[128,2048]{1,0:T(8,128)(2,1)}) %reduce-scatter.9.cloned.1.call-update) | async-done | bytes 524304 | tf_op jit(solution)/shard_map/reduce_scatter | solution.py:163
  475.0 1.9 fusion.41
  476.8 57.9 %all-reduce.2.cloned.1.call-done = bf16[256,2048]{1,0:T(8,128)(2,1)} async-done(((bf16[256,2048]{1,0:T(8,128)(2,1)}), bf16[256,2048]{1,0:T(8,128)(2,1)}) %all-reduce.2.cloned.1.call-update) | async-done | bytes 1048592 | tf_op jit(solution)/shard_map/psum | solution.py:140
  534.7 2.8 convert_element_type.123
  (59 shorter events, 2.1 us)
Async XLA Ops:
  7.2 21.8 %all-gather.8.cloned.1.call-start = ((), (), s32[]{:S(2)}) async-start(), calls=%async_computation.9 | async-start | bytes 1310720 | tf_op jit(solution)/shard_map/all_gather | solution.py:47
  7.9 40.1 %all-gather.6.cloned.1.call-start = ((), (), s32[]{:S(2)}) async-start(), calls=%async_computation.8 | async-start | bytes 1310720 | tf_op jit(solution)/shard_map/all_gather | solution.py:46
  9.8 120.6 %all-gather.10.cloned.1.call-start = ((), (), s32[]{:S(2)}) async-start(), calls=%async_computation.10 | async-start | bytes 5242880 | tf_op jit(solution)/shard_map/all_gather | solution.py:65
  10.5 187.5 %all-gather.12.cloned.1.call-start = ((), (), s32[]{:S(2)}) async-start(), calls=%async_computation.11 | async-start | bytes 5242880 | tf_op jit(solution)/shard_map/all_gather | solution.py:89
  30.5 21.0 %copy-start.6 = (bf16[512,1024]{0,1:T(8,128)(2,1)}, bf16[512,1024]{0,1:T(8,128)(2,1)S(1)}, u32[]{:S(2)}) copy-start(bf16[512,1024]{0,1:T(8,128)(2,1)S(1)} %copy.41) | copy-start | bytes 3145732
  50.1 1.4 copy-start
  51.5 82.0 %copy-start.8 = (f32[2048]{0:T(1024)S(1)}, f32[2048]{0:T(1024)}, u32[]{:S(2)}) copy-start(f32[2048]{0:T(1024)} %param.16) | copy-start | bytes 24580
  164.4 69.5 %all-gather.14.cloned.1.call-start = ((), (), s32[]{:S(2)}) async-start(), calls=%async_computation.13 | async-start | bytes 5242880 | tf_op jit(solution)/shard_map/all_gather | solution.py:108
  195.1 85.8 %reduce-scatter.5.cloned.1.call-start = ((), (), s32[]{:S(2)}) async-start(), calls=%async_computation.12 | async-start | bytes 5242880 | tf_op jit(solution)/shard_map/reduce_scatter | solution.py:95
  198.0 7.7 %copy-start.10 = (bf16[1,2048,1024]{2,1,0:T(8,128)(2,1)S(1)}, bf16[1,2048,1024]{2,1,0:T(8,128)(2,1)}, u32[]{:S(2)}) copy-start(bf16[1,2048,1024]{2,1,0:T(8,128)(2,1)} %param.18) | copy-start | bytes 12582916
  198.0 7.7 %copy-start.13 = (bf16[16,64,2048]{2,1,0:T(8,128)(2,1)S(1)}, bf16[16,64,2048]{2,1,0:T(8,128)(2,1)}, u32[]{:S(2)}) copy-start(bf16[16,64,2048]{2,1,0:T(8,128)(2,1)} %all-gather.12.cloned.1.call-done) | copy-start | bytes 12582916
  205.7 6.6 %copy-start.14 = (f32[1024,1024]{1,0:T(8,128)}, f32[1024,1024]{1,0:T(8,128)S(1)}, u32[]{:S(2)}) copy-start(f32[1024,1024]{1,0:T(8,128)S(1)} %fusion.11) | copy-start | bytes 12582916
  205.7 6.6 %copy-start.9 = (bf16[1,1024,2048]{2,1,0:T(8,128)(2,1)S(1)}, bf16[1,1024,2048]{2,1,0:T(8,128)(2,1)}, u32[]{:S(2)}) copy-start(bf16[1,1024,2048]{2,1,0:T(8,128)(2,1)} %param.19) | copy-start | bytes 12582916
  218.4 109.7 %reduce-scatter.7.cloned.1.call-start = ((), (), s32[]{:S(2)}) async-start(), calls=%async_computation.14 | async-start | bytes 5242880 | tf_op jit(solution)/shard_map/reduce_scatter | solution.py:119
  233.9 7.7 %copy-start.11 = (bf16[1,2048,1024]{2,1,0:T(8,128)(2,1)S(1)}, bf16[1,2048,1024]{2,1,0:T(8,128)(2,1)}, u32[]{:S(2)}) copy-start(bf16[1,2048,1024]{2,1,0:T(8,128)(2,1)} %param.18) | copy-start | bytes 12582916
  233.9 7.7 %copy-start.15 = (f32[1024,1024]{1,0:T(8,128)S(1)}, f32[1024,1024]{1,0:T(8,128)}, u32[]{:S(2)}) copy-start(f32[1024,1024]{1,0:T(8,128)} %copy-done.14) | copy-start | bytes 12582916
  241.7 6.9 %copy-start.16 = (f32[1024,1024]{1,0:T(8,128)}, f32[1024,1024]{1,0:T(8,128)S(1)}, u32[]{:S(2)}) copy-start(f32[1024,1024]{1,0:T(8,128)S(1)} %fusion.3) | copy-start | bytes 12582916
  241.7 6.9 %copy-start.12 = (bf16[1,2048,1024]{2,1,0:T(8,128)(2,1)S(1)}, bf16[1,2048,1024]{2,1,0:T(8,128)(2,1)}, u32[]{:S(2)}) copy-start(bf16[1,2048,1024]{2,1,0:T(8,128)(2,1)} %param.17) | copy-start | bytes 12582916
  280.9 47.2 %all-to-all-start.1 = ((bf16[4,64,2048]{2,1,0:T(8,128)(2,1)}), bf16[4,64,2048]{2,1,0:T(8,128)(2,1)S(1)}, u32[]{:S(2)}, u32[]{:S(2)}) async-start(bf16[4,64,2048]{2,1,0:T(8,128)(2,1)} %reduce-scatter.5.cloned.1.call-done), calls=%async_computation.2 | async-start | bytes 2097152 | tf_op jit(solution)/shard_map/all_to_all | solution.py:101
  328.1 30.1 %all-to-all-start.3 = ((bf16[4,64,2048]{2,1,0:T(8,128)(2,1)}), bf16[4,64,2048]{2,1,0:T(8,128)(2,1)S(1)}, u32[]{:S(2)}, u32[]{:S(2)}) async-start(bf16[4,64,2048]{2,1,0:T(8,128)(2,1)} %reduce-scatter.7.cloned.1.call-done), calls=%async_computation.5 | async-start | bytes 2097152 | tf_op jit(solution)/shard_map/all_to_all | solution.py:125
  332.7 107.5 %reduce-scatter.11.cloned.1.call-start = ((), (), s32[]{:S(2)}) async-start(), calls=%async_computation.16 | async-start | bytes 5242880 | tf_op jit(solution)/shard_map/reduce_scatter | solution.py:134
  359.2 2.7 copy-start.5
  361.9 3.5 copy-start.2
  365.0 5.0 copy-start.1
  365.1 109.9 %reduce-scatter.9.cloned.1.call-start = ((), (), s32[]{:S(2)}) async-start(), calls=%async_computation.15 | async-start | bytes 2621440 | tf_op jit(solution)/shard_map/reduce_scatter | solution.py:163
  370.1 4.8 copy-start.7
  376.8 1.8 copy-start.4
  378.5 61.6 %copy-start.3 = (bf16[512,1024]{0,1:T(8,128)(2,1)S(1)}, bf16[512,1024]{0,1:T(8,128)(2,1)}, u32[]{:S(2)}) copy-start(bf16[512,1024]{0,1:T(8,128)(2,1)} %all-gather.6.cloned.1.call-done) | copy-start | bytes 3145732
  381.4 153.3 %all-reduce.2.cloned.1.call-start = ((), (), s32[]{:S(2)}) async-start(), calls=%async_computation.17 | async-start | bytes 2097152 | tf_op jit(solution)/shard_map/psum | solution.py:140
Sparse Core Ops, SparseCore 0:
  9.5 19.4 all-gather.7
  31.1 16.8 all-gather.5
  49.5 80.7 all-gather.9
  164.5 33.4 all-gather.11
  199.4 34.4 all-gather.13
  236.3 44.5 reduce-scatter.4
  283.4 44.5 reduce-scatter.6
  365.2 74.9 reduce-scatter.10
  443.2 31.6 reduce-scatter.8
  478.0 56.6 all-reduce.1
where the time goes:
time: 545 us; the launch traced here: 544 us
  waiting for transfers between devices  366 us (67%)
  matrix products  68.7 us (13%)
  blocking collectives  57.4 us (11%)
  local copies, waits for them, and re-layouts  16.5 us (3%)
  between operations  14.4 us (3%)
  other arithmetic  11.2 us (2%)
  starting transfers between devices  9.97 us (2%)
    all_gather x1, waiting for transfers between devices, shards(): full_out = lax.all_gather(out_weight, 'expert', axis=0, tiled=True)  78.8 us
    reduce_scatter x1, waiting for transfers between devices, shards(): lax.psum_scatter(contract_first(attended, resid_grad).astype(jnp.bfloat16...  58.7 us
    psum x1, waiting for transfers between devices, shards(): weight_grad = lax.psum(grad_shard, ('section', 'dp')).astype(jnp.float32)  57.9 us
    reduce_scatter x1, waiting for transfers between devices, shards(): lax.psum_scatter(partial_grad.reshape(data_ways * experts, capacity, D).a...  42.6 us
    reduce_scatter x1, waiting for transfers between devices, shards(): lax.psum_scatter(jnp.concatenate([key_part.reshape(lax.axis_size('dp') *...  33.5 us
    dot_general x4, matrix products, contract_last(): lax.dot_general(left_side, right_side, (((1,), (1,)), ((), ())), preferre...  32.7 us
    all_to_all x1, blocking collectives, shards(): lax.all_to_all(send_buffer, 'expert', split_axis=0, concat_axis=0, tiled=...  29 us
    all_to_all x1, blocking collectives, shards(): lax.all_to_all(grad_buffer, 'expert', split_axis=0, concat_axis=0, tiled=...  28.4 us
  transfers between devices with their start and end apart: 12, of which 11 were waited for; matrix products, arithmetic and copies ran while one was open for 15% of the time, Pallas kernels for 0%

commit v1 on v0

--- a/solution.py
+++ b/solution.py
@@ -137,7 +137,7 @@
         scatter_dimension=0,
         tiled=True,
     )
-    weight_grad = lax.psum(grad_shard, ("section", "dp")).astype(jnp.float32)
+    weight_grad = lax.psum(lax.psum(grad_shard, "dp"), "section").astype(jnp.float32)
     grad_attended = contract_last(resid_grad, full_out).astype(jnp.bfloat16)
     grad_heads = grad_attended.reshape(tokens_here, HEADS, HEAD)
     grad_probs = jnp.einsum(

time: 545 us -> 566 us (1.039)
  waiting for transfers between devices: 366 us -> 388 us
    psum x1 -> x2, waiting for transfers between devices: 57.9 us -> 75.1 us  [the longest x1 40.6 us: shards(): lax.psum(lax.psum(grad_shard, 'dp'), 'section').astype(jnp.float32)]
  transfers between devices with their start and end apart: 12 -> 13, of which waited for: 11 -> 12; matrix products, arithmetic and copies ran while one was open for 15% -> 14% of each run, Pallas kernels for 0% -> 0%
where the time goes in v1:
time: 566 us
  waiting for transfers between devices  388 us (69%)
  matrix products  68.7 us (12%)
  blocking collectives  57.4 us (10%)
  local copies, waits for them, and re-layouts  16.5 us (3%)
  between operations  14.1 us (2%)
  other arithmetic  11.1 us (2%)
  starting transfers between devices  10 us (2%)
    all_gather x1, waiting for transfers between devices, shards(): full_out = lax.all_gather(out_weight, 'expert', axis=0, tiled=True)  78.8 us
    reduce_scatter x1, waiting for transfers between devices, shards(): lax.psum_scatter(contract_first(attended, resid_grad).astype(jnp.bfloat16...  63.3 us
    reduce_scatter x1, waiting for transfers between devices, shards(): lax.psum_scatter(partial_grad.reshape(data_ways * experts, capacity, D).a...  42.6 us
    psum x1, waiting for transfers between devices, shards(): lax.psum(lax.psum(grad_shard, 'dp'), 'section').astype(jnp.float32)  40.6 us
    psum x1, waiting for transfers between devices, shards(): lax.psum(grad_shard, 'dp')  34.5 us
    reduce_scatter x1, waiting for transfers between devices, shards(): lax.psum_scatter(jnp.concatenate([key_part.reshape(lax.axis_size('dp') *...  33.3 us
    dot_general x4, matrix products, contract_last(): lax.dot_general(left_side, right_side, (((1,), (1,)), ((), ())), preferre...  32.7 us
    all_to_all x1, blocking collectives, shards(): lax.all_to_all(send_buffer, 'expert', split_axis=0, concat_axis=0, tiled=...  29 us
  transfers between devices with their start and end apart: 13, of which 12 were waited for; matrix products, arithmetic and copies ran while one was open for 14% of the time, Pallas kernels for 0%

profile of v1, /device:TPU:0, one launch (start us, length us, event | category | flops | bytes accessed | tf_op | source)
XLA Modules:
  0.0 565.7 jit_solution(1721976271273994731)
XLA Ops:
  7.2 0.7 all-gather.8.cloned.1.call-update
  7.9 1.8 copy.38
  9.8 0.7 all-gather.10.cloned.1.call-update
  10.5 1.1 copy.51
  11.7 0.9 fusion.22
  12.6 0.7 fusion.37
  13.2 15.7 %all-gather.8.cloned.1.call-done = bf16[512,1024]{1,0:T(8,128)(2,1)} async-done(((bf16[128,1024]{1,0:T(8,128)(2,1)}), bf16[512,1024]{1,0:T(8,128)(2,1)}) %all-gather.8.cloned.1.call-update) | async-done | bytes 1048592 | tf_op jit(solution)/shard_map/all_gather | solution.py:47
  29.0 1.5 copy.41
  30.5 17.5 %all-gather.6.cloned.1.call-done = bf16[512,1024]{0,1:T(8,128)(2,1)} async-done(((bf16[128,1024]{0,1:T(8,128)(2,1)}), bf16[512,1024]{0,1:T(8,128)(2,1)}) %all-gather.6.cloned.1.call-update) | async-done | bytes 1048592 | tf_op jit(solution)/shard_map/all_gather | solution.py:46
  48.0 2.1 fusion.42
  50.1 1.4 convolution_convert_fusion.2
  51.5 78.8 %all-gather.10.cloned.1.call-done = bf16[1024,2048]{1,0:T(8,128)(2,1)} async-done(((bf16[256,2048]{1,0:T(8,128)(2,1)}), bf16[1024,2048]{1,0:T(8,128)(2,1)}) %all-gather.10.cloned.1.call-update) | async-done | bytes 4194320 | tf_op jit(solution)/shard_map/all_gather | solution.py:65
  130.3 3.2 multiply_reduce_fusion.3
  133.5 1.8 scatter_custom_fusion
  135.3 29.0 %all_to_all.20 = bf16[4,64,2048]{2,1,0:T(8,128)(2,1)} all-to-all(bf16[4,64,2048]{2,1,0:T(8,128)(2,1)S(1)} %bitcast.80), channel_id=1, replica_groups=mesh['section'=2,'expert'=4,'dp'=4] {'expert'}, dimensions={0} | all-to-all | bytes 2097152 | tf_op jit(solution)/shard_map/all_to_all | solution.py:87
  164.4 2.2 scatter_custom_fusion.1
  166.6 28.4 %all_to_all.21 = bf16[4,64,2048]{2,1,0:T(8,128)(2,1)} all-to-all(bf16[4,64,2048]{2,1,0:T(8,128)(2,1)S(1)} %bitcast.78), channel_id=1, replica_groups=mesh['section'=2,'expert'=4,'dp'=4] {'expert'}, dimensions={0} | all-to-all | bytes 2097152 | tf_op jit(solution)/shard_map/all_to_all | solution.py:107
  195.1 2.9 all-gather.12.cloned.1.call-done
  198.0 7.6 %fusion.11 = f32[1024,1024]{1,0:T(8,128)S(1)} fusion(bf16[1024,2048]{1,0:T(8,128)(2,1)} %bitcast.94, bf16[1,2048,1024]{2,1,0:T(8,128)(2,1)} %param.17), kind=kOutput, calls=%fused_computation.16 | convolution fusion | flops 4294967296 | bytes 12582912 | tf_op jit(solution)/shard_map/dot_general | solution.py:91
  205.7 6.5 %multiply_convert_fusion.2 = (bf16[1024,1024]{1,0:T(8,128)(2,1)S(1)}, f32[1024,1024]{1,0:T(8,128)}) fusion(f32[1024,1024]{1,0:T(8,128)S(1)} %fusion.11, bf16[1024,2048]{1,0:T(8,128)(2,1)S(1)} %bitcast.95, bf16[1,2048,1024]{2,1,0:T(8,128)(2,1)S(1)} %copy-done.10), kind=kOutput, calls=%fused_computation.20 | convolution fusion | flops 4301258752 | bytes 18874368 | tf_op jit(solution)/shard_map/dot_general | solution.py:92
  212.2 6.1 %fusion.14 = bf16[16,64,2048]{2,1,0:T(8,128)(2,1)} fusion(bf16[16,64,1024]{2,1,0:T(8,128)(2,1)S(1)} %bitcast.97, bf16[1,1024,2048]{2,1,0:T(8,128)(2,1)S(1)} %copy-done.9), kind=kOutput, calls=%fused_computation.24 | convolution fusion | flops 4297064448 | bytes 10485760 | tf_op jit(solution)/shard_map/dot_general | solution.py:94
  218.6 15.3 %all-gather.14.cloned.1.call-done = bf16[16,64,2048]{2,1,0:T(8,128)(2,1)} async-done(((bf16[4,64,2048]{2,1,0:T(8,128)(2,1)}), bf16[16,64,2048]{2,1,0:T(8,128)(2,1)}) %all-gather.14.cloned.1.call-update) | async-done | bytes 4194320 | tf_op jit(solution)/shard_map/all_gather | solution.py:108
  233.9 7.7 %fusion.3 = f32[1024,1024]{1,0:T(8,128)S(1)} fusion(bf16[1024,2048]{1,0:T(8,128)(2,1)} %bitcast.93, bf16[1,1024,2048]{2,1,0:T(8,128)(2,1)} %param.19), kind=kOutput, calls=%fused_computation.8 | convolution fusion | flops 4294967296 | bytes 12582912 | tf_op jit(solution)/shard_map/dot_general | solution.py:16
  241.7 6.9 %fusion.5 = f32[1024,2048]{1,0:T(8,128)} fusion(bf16[1,2048,1024]{2,1,0:T(8,128)(2,1)S(1)} %copy-done.11, f32[1024,1024]{1,0:T(8,128)S(1)} %fusion.3, f32[1024,1024]{1,0:T(8,128)S(1)} %copy-done.15), kind=kOutput, calls=%fused_computation.10 | convolution fusion | flops 4301258752 | bytes 20971520 | tf_op jit(solution)/shard_map/dot_general | solution.py:16
  248.5 14.3 %add_convert_fusion = bf16[1024,2048]{1,0:T(8,128)(2,1)} fusion(f32[1024,2048]{1,0:T(8,128)} %fusion.5, bf16[1,2048,1024]{2,1,0:T(8,128)(2,1)S(1)} %copy-done.12, f32[1024,1024]{1,0:T(8,128)} %copy-done.14, f32[1024,1024]{1,0:T(8,128)} %copy-done.16, f32[1024,1024]{1,0:T(8,128)} %get-tuple-element.33), kind=kOutput, calls=%fused_computation.5 | convolution fusion | flops 4309647360 | bytes 29360128 | tf_op jit(solution)/shard_map/dot_general | solution.py:16
  262.9 18.0 %reduce-scatter.5.cloned.1.call-done = bf16[4,64,2048]{2,1,0:T(8,128)(2,1)} async-done(((bf16[16,64,2048]{2,1,0:T(8,128)(2,1)}), bf16[4,64,2048]{2,1,0:T(8,128)(2,1)}) %reduce-scatter.5.cloned.1.call-update) | async-done | bytes 1048592 | tf_op jit(solution)/shard_map/reduce_scatter | solution.py:95
  280.9 4.6 all-to-all-start.1
  285.5 42.6 %reduce-scatter.7.cloned.1.call-done = bf16[4,64,2048]{2,1,0:T(8,128)(2,1)} async-done(((bf16[16,64,2048]{2,1,0:T(8,128)(2,1)}), bf16[4,64,2048]{2,1,0:T(8,128)(2,1)}) %reduce-scatter.7.cloned.1.call-update) | async-done | bytes 1048592 | tf_op jit(solution)/shard_map/reduce_scatter | solution.py:119
  328.1 4.6 all-to-all-start.3
  332.7 1.7 gather_fusion
  334.4 23.8 %all-to-all-done.3 = bf16[4,64,2048]{2,1,0:T(8,128)(2,1)S(1)} async-done(((bf16[4,64,2048]{2,1,0:T(8,128)(2,1)}), bf16[4,64,2048]{2,1,0:T(8,128)(2,1)S(1)}, u32[]{:S(2)}, u32[]{:S(2)}) %all-to-all-start.3) | async-done | bytes 1048608 | tf_op jit(solution)/shard_map/all_to_all | solution.py:125
  358.2 0.9 gather_fusion.1
  359.5 2.4 add_convert_fusion.1
  361.9 3.2 convolution_convert_fusion
  365.3 3.9 convolution_convert_fusion.3
  369.2 0.8 copy.52
  370.1 2.5 convolution_convert_fusion.1
  372.6 2.3 copy.47
  374.9 1.5 multiply_reduce_fusion
  376.8 63.3 %reduce-scatter.11.cloned.1.call-done = bf16[256,2048]{1,0:T(8,128)(2,1)} async-done(((bf16[1024,2048]{1,0:T(8,128)(2,1)}), bf16[256,2048]{1,0:T(8,128)(2,1)}) %reduce-scatter.11.cloned.1.call-update) | async-done | bytes 1048592 | tf_op jit(solution)/shard_map/reduce_scatter | solution.py:134
  440.6 1.3 copy.46
  442.0 2.8 pad_maximum_fusion
  444.9 34.5 %all-reduce.3.cloned.1.call-done = bf16[256,2048]{1,0:T(8,128)(2,1)} async-done(((bf16[256,2048]{1,0:T(8,128)(2,1)}), bf16[256,2048]{1,0:T(8,128)(2,1)}) %all-reduce.3.cloned.1.call-update) | async-done | bytes 1048592 | tf_op jit(solution)/shard_map/psum | solution.py:140
  479.8 0.9 copy.48
  480.7 33.3 %reduce-scatter.9.cloned.1.call-done = bf16[128,2048]{1,0:T(8,128)(2,1)} async-done(((bf16[512,2048]{1,0:T(8,128)(2,1)}), bf16[128,2048]{1,0:T(8,128)(2,1)}) %reduce-scatter.9.cloned.1.call-update) | async-done | bytes 524304 | tf_op jit(solution)/shard_map/reduce_scatter | solution.py:163
  514.0 1.9 fusion.41
  515.8 40.6 %all-reduce.5.cloned.1.call-done = bf16[256,2048]{1,0:T(8,128)(2,1)} async-done(((bf16[256,2048]{1,0:T(8,128)(2,1)}), bf16[256,2048]{1,0:T(8,128)(2,1)}) %all-reduce.5.cloned.1.call-update) | async-done | bytes 1048592 | tf_op jit(solution)/shard_map/psum | solution.py:140
  556.4 2.8 convert_element_type.123
  (62 shorter events, 2.6 us)
Async XLA Ops:
  7.2 21.8 %all-gather.8.cloned.1.call-start = ((), (), s32[]{:S(2)}) async-start(), calls=%async_computation.9 | async-start | bytes 1310720 | tf_op jit(solution)/shard_map/all_gather | solution.py:47
  7.9 40.1 %all-gather.6.cloned.1.call-start = ((), (), s32[]{:S(2)}) async-start(), calls=%async_computation.8 | async-start | bytes 1310720 | tf_op jit(solution)/shard_map/all_gather | solution.py:46
  9.8 120.6 %all-gather.10.cloned.1.call-start = ((), (), s32[]{:S(2)}) async-start(), calls=%async_computation.10 | async-start | bytes 5242880 | tf_op jit(solution)/shard_map/all_gather | solution.py:65
  10.5 187.5 %all-gather.12.cloned.1.call-start = ((), (), s32[]{:S(2)}) async-start(), calls=%async_computation.11 | async-start | bytes 5242880 | tf_op jit(solution)/shard_map/all_gather | solution.py:89
  30.5 21.0 %copy-start.6 = (bf16[512,1024]{0,1:T(8,128)(2,1)}, bf16[512,1024]{0,1:T(8,128)(2,1)S(1)}, u32[]{:S(2)}) copy-start(bf16[512,1024]{0,1:T(8,128)(2,1)S(1)} %copy.41) | copy-start | bytes 3145732
  50.1 1.4 copy-start
  51.5 82.0 %copy-start.8 = (f32[2048]{0:T(1024)S(1)}, f32[2048]{0:T(1024)}, u32[]{:S(2)}) copy-start(f32[2048]{0:T(1024)} %param.16) | copy-start | bytes 24580
  164.4 69.5 %all-gather.14.cloned.1.call-start = ((), (), s32[]{:S(2)}) async-start(), calls=%async_computation.13 | async-start | bytes 5242880 | tf_op jit(solution)/shard_map/all_gather | solution.py:108
  195.1 85.8 %reduce-scatter.5.cloned.1.call-start = ((), (), s32[]{:S(2)}) async-start(), calls=%async_computation.12 | async-start | bytes 5242880 | tf_op jit(solution)/shard_map/reduce_scatter | solution.py:95
  198.0 7.7 %copy-start.10 = (bf16[1,2048,1024]{2,1,0:T(8,128)(2,1)S(1)}, bf16[1,2048,1024]{2,1,0:T(8,128)(2,1)}, u32[]{:S(2)}) copy-start(bf16[1,2048,1024]{2,1,0:T(8,128)(2,1)} %param.18) | copy-start | bytes 12582916
  198.0 7.7 %copy-start.13 = (bf16[16,64,2048]{2,1,0:T(8,128)(2,1)S(1)}, bf16[16,64,2048]{2,1,0:T(8,128)(2,1)}, u32[]{:S(2)}) copy-start(bf16[16,64,2048]{2,1,0:T(8,128)(2,1)} %all-gather.12.cloned.1.call-done) | copy-start | bytes 12582916
  205.7 6.6 %copy-start.14 = (f32[1024,1024]{1,0:T(8,128)}, f32[1024,1024]{1,0:T(8,128)S(1)}, u32[]{:S(2)}) copy-start(f32[1024,1024]{1,0:T(8,128)S(1)} %fusion.11) | copy-start | bytes 12582916
  205.7 6.6 %copy-start.9 = (bf16[1,1024,2048]{2,1,0:T(8,128)(2,1)S(1)}, bf16[1,1024,2048]{2,1,0:T(8,128)(2,1)}, u32[]{:S(2)}) copy-start(bf16[1,1024,2048]{2,1,0:T(8,128)(2,1)} %param.19) | copy-start | bytes 12582916
  218.4 109.7 %reduce-scatter.7.cloned.1.call-start = ((), (), s32[]{:S(2)}) async-start(), calls=%async_computation.14 | async-start | bytes 5242880 | tf_op jit(solution)/shard_map/reduce_scatter | solution.py:119
  233.9 7.7 %copy-start.11 = (bf16[1,2048,1024]{2,1,0:T(8,128)(2,1)S(1)}, bf16[1,2048,1024]{2,1,0:T(8,128)(2,1)}, u32[]{:S(2)}) copy-start(bf16[1,2048,1024]{2,1,0:T(8,128)(2,1)} %param.18) | copy-start | bytes 12582916
  233.9 7.7 %copy-start.15 = (f32[1024,1024]{1,0:T(8,128)S(1)}, f32[1024,1024]{1,0:T(8,128)}, u32[]{:S(2)}) copy-start(f32[1024,1024]{1,0:T(8,128)} %copy-done.14) | copy-start | bytes 12582916
  241.7 6.9 %copy-start.16 = (f32[1024,1024]{1,0:T(8,128)}, f32[1024,1024]{1,0:T(8,128)S(1)}, u32[]{:S(2)}) copy-start(f32[1024,1024]{1,0:T(8,128)S(1)} %fusion.3) | copy-start | bytes 12582916
  241.7 6.9 %copy-start.12 = (bf16[1,2048,1024]{2,1,0:T(8,128)(2,1)S(1)}, bf16[1,2048,1024]{2,1,0:T(8,128)(2,1)}, u32[]{:S(2)}) copy-start(bf16[1,2048,1024]{2,1,0:T(8,128)(2,1)} %param.17) | copy-start | bytes 12582916
  280.9 47.2 %all-to-all-start.1 = ((bf16[4,64,2048]{2,1,0:T(8,128)(2,1)}), bf16[4,64,2048]{2,1,0:T(8,128)(2,1)S(1)}, u32[]{:S(2)}, u32[]{:S(2)}) async-start(bf16[4,64,2048]{2,1,0:T(8,128)(2,1)} %reduce-scatter.5.cloned.1.call-done), calls=%async_computation.2 | async-start | bytes 2097152 | tf_op jit(solution)/shard_map/all_to_all | solution.py:101
  328.1 30.1 %all-to-all-start.3 = ((bf16[4,64,2048]{2,1,0:T(8,128)(2,1)}), bf16[4,64,2048]{2,1,0:T(8,128)(2,1)S(1)}, u32[]{:S(2)}, u32[]{:S(2)}) async-start(bf16[4,64,2048]{2,1,0:T(8,128)(2,1)} %reduce-scatter.7.cloned.1.call-done), calls=%async_computation.5 | async-start | bytes 2097152 | tf_op jit(solution)/shard_map/all_to_all | solution.py:125
  332.7 107.5 %reduce-scatter.11.cloned.1.call-start = ((), (), s32[]{:S(2)}) async-start(), calls=%async_computation.16 | async-start | bytes 5242880 | tf_op jit(solution)/shard_map/reduce_scatter | solution.py:134
  359.2 2.7 copy-start.5
  361.9 3.5 copy-start.2
  365.0 5.0 copy-start.1
  365.1 114.3 %all-reduce.3.cloned.1.call-start = ((), (), s32[]{:S(2)}) async-start(), calls=%async_computation.17 | async-start | bytes 2097152 | tf_op jit(solution)/shard_map/psum | solution.py:140
  370.1 4.8 copy-start.7
  376.8 65.2 %copy-start.4 = (bf16[512,1024]{1,0:T(8,128)(2,1)S(1)}, bf16[512,1024]{1,0:T(8,128)(2,1)}, u32[]{:S(2)}) copy-start(bf16[512,1024]{1,0:T(8,128)(2,1)} %copy.47) | copy-start | bytes 3145732
  440.2 73.8 %reduce-scatter.9.cloned.1.call-start = ((), (), s32[]{:S(2)}) async-start(), calls=%async_computation.15 | async-start | bytes 2621440 | tf_op jit(solution)/shard_map/reduce_scatter | solution.py:163
  442.0 37.4 %copy-start.3 = (bf16[512,1024]{0,1:T(8,128)(2,1)S(1)}, bf16[512,1024]{0,1:T(8,128)(2,1)}, u32[]{:S(2)}) copy-start(bf16[512,1024]{0,1:T(8,128)(2,1)} %all-gather.6.cloned.1.call-done) | copy-start | bytes 3145732
  444.8 111.6 %all-reduce.5.cloned.1.call-start = ((), (), s32[]{:S(2)}) async-start(), calls=%async_computation.18 | async-start | bytes 2097152 | tf_op jit(solution)/shard_map/psum | solution.py:140
Sparse Core Ops, SparseCore 0:
  9.5 19.4 all-gather.7
  31.1 16.8 all-gather.5
  49.5 80.7 all-gather.9
  164.5 33.4 all-gather.11
  199.4 34.4 all-gather.13
  236.3 44.5 reduce-scatter.4
  283.4 44.5 reduce-scatter.6
  365.2 74.9 reduce-scatter.10
  442.5 36.8 all-reduce.2
  482.3 31.6 reduce-scatter.8
  516.3 40.0 all-reduce.4
